TPU v7x, 32 devices: a whole 2x2x4 slice. The times are simulated.
32 devices in a mesh: snp: 8 (over z, x), trait: 4 (over y, core).
Axes of the slice: x: 2, y: 2, z: 4, core: 2. Of those that a mesh axis runs over, the one named last changes fastest.
Arguments:
- genotype: bfloat16 [32, 8192], P(None, 'snp'), may hold values from -0.0625 to 0.0625
- targets: bfloat16 [32, 16384], P('snp', 'trait'), may hold values from -6 to 6
- effect_sizes: float32 [8192, 16384], P('snp', 'trait'), may hold values from -6 to 6
- membership: int32 [4, 128, 128], replicated, may hold values from 0 to 1, as said below
- node_weight: float32 [4, 128], replicated, may hold values from 0.03 to 1
Outputs:
- updated: float32 [8192, 16384], P('snp', 'trait')
Inputs may be any that keep to these rules, and one draw needn't show every extreme that they name: `membership`: at each level the node slots 0 .. c - 1 partition all 128 trait blocks, the remaining slots cover none; every node of a level lies inside one node of the next level; at level 0 each block is its own node.
All inputs are finite; a program needn't handle non-finite values.
Results may differ from a plain program's by a relative error of at most 0.00042.
Values may be sent and summed in bfloat16 or wider, within the bound.
A program may use at most 128 MiB of HBM per device.

v0:
```python
import jax
import jax.numpy as jnp
from jax import lax
from jax.sharding import PartitionSpec as P

TB = 128
LEVELS = 4
step_size = 0.5


def factor_of(node_sq, threshold):
    norm = jnp.sqrt(node_sq)
    return jnp.maximum(norm - threshold, 0.0) / jnp.maximum(norm, threshold)


def shrink_local(value, membership, node_weight):
    local_blocks = value.shape[1] // TB
    first_block = lax.axis_index("trait") * local_blocks
    for level in range(LEVELS):
        member_all = membership[level].astype(jnp.float32)
        count = jnp.sum(member_all, axis=1)
        threshold = step_size * node_weight[level] * jnp.sqrt(TB * jnp.maximum(count, 1.0))
        member = lax.dynamic_slice_in_dim(member_all, first_block, local_blocks, 1)
        blocks = value.reshape(value.shape[0], local_blocks, TB)
        block_sq = jnp.sum(blocks * blocks, axis=2)
        partial_sq = jnp.dot(block_sq, member.T, precision=lax.Precision.HIGHEST)
        node_sq = lax.psum(partial_sq, "trait")
        factor = factor_of(node_sq, threshold)
        block_factor = jnp.dot(factor, member, precision=lax.Precision.HIGHEST)
        value = (blocks * block_factor[:, :, None]).reshape(value.shape)
    return value


def body(genotype, targets, effect_sizes, membership, node_weight):
    current = effect_sizes
    targets_full = lax.all_gather(targets, "snp", axis=0, tiled=True)
    current_bf = current.astype(jnp.bfloat16)
    fitted = lax.psum(jnp.dot(genotype, current_bf, preferred_element_type=jnp.float32), "snp")
    residual = (targets_full.astype(jnp.float32) - fitted).astype(jnp.bfloat16)
    gradient = lax.dot_general(
        genotype, residual, (((0,), (0,)), ((), ())), preferred_element_type=jnp.float32
    )
    current = shrink_local(current + step_size * gradient, membership, node_weight)
    return current


def solution(mesh):
    return jax.shard_map(
        body,
        mesh=mesh,
        in_specs=(P(None, "snp"), P("snp", "trait"), P("snp", "trait"), P(), P()),
        out_specs=P("snp", "trait"),
        check_vma=False,
    )
```

profile of v0, /device:TPU:0, one launch (start us, length us, event | category | flops | bytes accessed | tf_op | source)
XLA Modules:
  0.0 313.8 jit_solution(9431012328404320103)
XLA Ops:
  6.5 0.8 copy-done
  7.4 8.1 %fusion = f32[32,4096]{1,0:T(8,128)} fusion(bf16[32,1024]{1,0:T(8,128)(2,1)S(1)} %copy-done, f32[1024,4096]{1,0:T(8,128)} %param.7), kind=kOutput, calls=%fused_computation.9 | convolution fusion | flops 272629760 | bytes 17367040 | tf_op jit(solution)/shard_map/dot_general | solution.py:38
  15.6 17.5 %copy.8 = f32[1024,4096]{0,1:T(8,128)} copy(f32[1024,4096]{1,0:T(8,128)} %param.7) | data formatting | bytes 33554432 | tf_op args[2]
  33.1 32.6 %all-gather = bf16[8,4,4096]{2,1,0:T(4,128)(2,1)S(1)} all-gather(bf16[1,4,4096]{2,1,0:T(4,128)(2,1)S(1)} %bitcast.72), channel_id=1, replica_groups=mesh['snp'=8,'trait'=4] {'snp'}, dimensions={0}, use_global_device_ids=true | all-gather | bytes 294912 | tf_op jit(solution)/shard_map/all_gather | solution.py:36
  65.8 25.0 %all-reduce.6.cloned.1.call-done = f32[32,4096]{1,0:T(8,128)} async-done(((f32[32,4096]{1,0:T(8,128)}), f32[32,4096]{1,0:T(8,128)}) %all-reduce.6.cloned.1.call-update) | async-done | bytes 524304 | tf_op jit(solution)/shard_map/psum | solution.py:38
  90.8 11.0 %multiply_reduce_fusion.3 = (f32[1024,32]{0,1:T(8,128)S(1)}, f32[1024,4096]{0,1:T(8,128)}) fusion(f32[1024,4096]{0,1:T(8,128)} %copy.8, bf16[32,1024]{1,0:T(8,128)(2,1)S(1)} %copy-done, f32[32,4096]{1,0:T(8,128)S(1)} %reshape.95, f32[32,4096]{1,0:T(8,128)} %all-reduce.6.cloned.1.call-done), kind=kOutput, calls=%fused_computation.8 | convolution fusion | flops 285442048 | bytes 34799616 | tf_op jit(solution)/shard_map/dot_general | solution.py:40
  101.8 1.8 fusion.24
  103.9 32.4 %all-reduce.8.cloned.1.call-done = f32[1024,128]{1,0:T(8,128)} async-done(((f32[1024,128]{1,0:T(8,128)}), f32[1024,128]{1,0:T(8,128)}) %all-reduce.8.cloned.1.call-update) | async-done | bytes 524304 | tf_op jit(solution)/shard_map/psum | solution.py:27
  136.3 1.8 fusion.2
  138.2 8.5 %multiply_reduce_fusion.2 = f32[1024,32]{0,1:T(8,128)S(1)} fusion(f32[1024,4096]{0,1:T(8,128)} %get-tuple-element.18, f32[1024,32]{0,1:T(8,128)S(1)} %fusion.2), kind=kLoop, calls=%fused_computation.7 | loop fusion | flops 12550144 | bytes 17039360 | tf_op jit(solution)/shard_map/reduce_sum | solution.py:25
  146.7 1.9 fusion.21
  148.8 33.1 %all-reduce.10.cloned.1.call-done = f32[1024,128]{1,0:T(8,128)} async-done(((f32[1024,128]{1,0:T(8,128)}), f32[1024,128]{1,0:T(8,128)}) %all-reduce.10.cloned.1.call-update) | async-done | bytes 524304 | tf_op jit(solution)/shard_map/psum | solution.py:27
  181.9 1.8 fusion.3
  183.7 9.5 %multiply_reduce_fusion.1 = f32[1024,32]{0,1:T(8,128)S(1)} fusion(f32[1024,4096]{0,1:T(8,128)} %get-tuple-element.18, f32[1024,32]{0,1:T(8,128)S(1)} %fusion.3, f32[1024,32]{0,1:T(8,128)S(1)} %fusion.2), kind=kLoop, calls=%fused_computation.6 | loop fusion | flops 16744448 | bytes 17170432 | tf_op jit(solution)/shard_map/reduce_sum | solution.py:25
  193.2 1.9 fusion.18
  195.1 0.3 all-reduce.14.cloned.1.call-start
  195.4 33.1 %all-reduce.12.cloned.1.call-done = f32[1024,128]{1,0:T(8,128)} async-done(((f32[1024,128]{1,0:T(8,128)}), f32[1024,128]{1,0:T(8,128)}) %all-reduce.12.cloned.1.call-update) | async-done | bytes 524304 | tf_op jit(solution)/shard_map/psum | solution.py:27
  228.4 1.8 fusion.4
  230.2 10.6 %multiply_reduce_fusion = f32[1024,32]{0,1:T(8,128)S(1)} fusion(f32[1024,4096]{0,1:T(8,128)} %get-tuple-element.18, f32[1024,32]{0,1:T(8,128)S(1)} %fusion.4, f32[1024,32]{0,1:T(8,128)S(1)} %fusion.3, f32[1024,32]{0,1:T(8,128)S(1)} %fusion.2), kind=kLoop, calls=%fused_computation.5 | loop fusion | flops 20938752 | bytes 17301504 | tf_op jit(solution)/shard_map/reduce_sum | solution.py:25
  240.8 1.9 fusion.15
  242.7 33.3 %all-reduce.14.cloned.1.call-done = f32[1024,128]{1,0:T(8,128)} async-done(((f32[1024,128]{1,0:T(8,128)}), f32[1024,128]{1,0:T(8,128)}) %all-reduce.14.cloned.1.call-update) | async-done | bytes 524304 | tf_op jit(solution)/shard_map/psum | solution.py:27
  276.0 1.8 fusion.5
  277.9 12.0 %bitcast_multiply_fusion = f32[1024,4096]{0,1:T(8,128)} fusion(f32[1024,4096]{0,1:T(8,128)} %get-tuple-element.18, f32[1024,32]{0,1:T(8,128)S(1)} %fusion.5, f32[1024,32]{0,1:T(8,128)S(1)} %fusion.4, f32[1024,32]{0,1:T(8,128)S(1)} %fusion.3, f32[1024,32]{0,1:T(8,128)S(1)} %fusion.2), kind=kLoop, calls=%fused_computation | loop fusion | flops 16777216 | bytes 34078720 | tf_op jit(solution)/shard_map/mul | solution.py:30
  289.9 17.4 %copy.9 = f32[1024,4096]{1,0:T(8,128)} copy(f32[1024,4096]{0,1:T(8,128)} %bitcast_multiply_fusion) | data formatting | bytes 33554432 | tf_op jit(solution)/shard_map/mul | solution.py:30
  (22 shorter events, 0.6 us)
Async XLA Ops:
  6.5 0.8 copy-start
  6.5 84.3 %all-reduce.6.cloned.1.call-start = ((), (), s32[]{:S(2)}) async-start(), calls=%async_computation | async-start | bytes 1048576 | tf_op jit(solution)/shard_map/psum | solution.py:38
  15.5 120.8 %all-reduce.8.cloned.1.call-start = ((), (), s32[]{:S(2)}) async-start(), calls=%async_computation.1 | async-start | bytes 1048576 | tf_op jit(solution)/shard_map/psum | solution.py:27
  15.6 17.5 %copy-start.3 = (bf16[4,4096]{1,0:T(4,128)(2,1)S(1)}, bf16[4,4096]{1,0:T(4,128)(2,1)}, u32[]{:S(2)}) copy-start(bf16[4,4096]{1,0:T(4,128)(2,1)} %param.6) | copy-start | bytes 98308
  15.6 50.2 %copy-start.2 = (s32[4,128,128]{2,1,0:T(8,128)S(1)}, s32[4,128,128]{2,1,0:T(8,128)}, u32[]{:S(2)}) copy-start(s32[4,128,128]{2,1,0:T(8,128)} %param.8) | copy-start | bytes 786436
  65.8 38.1 %copy-start.4 = (f32[4,128]{1,0:T(4,128)S(1)}, f32[4,128]{1,0:T(4,128)}, u32[]{:S(2)}) copy-start(f32[4,128]{1,0:T(4,128)} %param.9) | copy-start | bytes 6148
  103.7 78.2 %all-reduce.10.cloned.1.call-start = ((), (), s32[]{:S(2)}) async-start(), calls=%async_computation.2 | async-start | bytes 1048576 | tf_op jit(solution)/shard_map/psum | solution.py:27
  148.6 79.8 %all-reduce.12.cloned.1.call-start = ((), (), s32[]{:S(2)}) async-start(), calls=%async_computation.3 | async-start | bytes 1048576 | tf_op jit(solution)/shard_map/psum | solution.py:27
  195.1 80.9 %all-reduce.14.cloned.1.call-start = ((), (), s32[]{:S(2)}) async-start(), calls=%async_computation.4 | async-start | bytes 1048576 | tf_op jit(solution)/shard_map/psum | solution.py:27
  277.9 29.4 %copy-start.1 = (bf16[32,1024]{1,0:T(8,128)(2,1)S(1)}, bf16[32,1024]{1,0:T(8,128)(2,1)}, u32[]{:S(2)}) copy-start(bf16[32,1024]{1,0:T(8,128)(2,1)} %param.5) | copy-start | bytes 196612
Sparse Core Ops, SparseCore 0:
  15.6 75.1 all-reduce.5
  103.8 32.4 all-reduce.7
  148.7 33.1 all-reduce.9
  195.2 33.1 all-reduce.11
  242.8 33.1 all-reduce.13
where the time goes:
time: 315 us; the launch traced here: 314 us
  waiting for transfers between devices  157 us (50%)
  other arithmetic  40.7 us (13%)
  local copies, waits for them, and re-layouts  35.8 us (11%)
  matrix products  33.9 us (11%)
  blocking collectives  32.6 us (10%)
  between operations  13.3 us (4%)
    psum x4, waiting for transfers between devices, shrink_local(): node_sq = lax.psum(partial_sq, 'trait')  132 us
    all_gather x1, blocking collectives, body(): targets_full = lax.all_gather(targets, 'snp', axis=0, tiled=True)  32.6 us
    reduce_sum x3, other arithmetic, shrink_local(): block_sq = jnp.sum(blocks * blocks, axis=2)  28.6 us
    psum x1, waiting for transfers between devices, body(): lax.psum(jnp.dot(genotype, current_bf, preferred_element_type=jnp.float32...  25 us
    unnamed x11, local copies, waits for them, and re-layouts  18.4 us
    mul x1, local copies, waits for them, and re-layouts, shrink_local(): value = (blocks * block_factor[:, :, None]).reshape(value.shape)  17.4 us
    mul x1, other arithmetic, shrink_local(): value = (blocks * block_factor[:, :, None]).reshape(value.shape)  12 us
    dot_general x1, matrix products, body(): lax.dot_general(genotype, residual, (((0,), (0,)), ((), ())), preferred_e...  11 us
  transfers between devices with their start and end apart: 5, of which 5 were waited for; matrix products, arithmetic and copies ran while one was open for 6% of the time, Pallas kernels for 0%

commit v1 on v0

--- a/solution.py
+++ b/solution.py
@@ -6,6 +6,12 @@
 TB = 128
 LEVELS = 4
 step_size = 0.5
+
+
+def joined_along(parts, dim):
+    parts = jnp.moveaxis(parts, 0, dim)
+    shape = parts.shape
+    return parts.reshape(*shape[:dim], shape[dim] * shape[dim + 1], *shape[dim + 2 :])
 
 
 def factor_of(node_sq, threshold):
@@ -33,7 +39,19 @@
 
 def body(genotype, targets, effect_sizes, membership, node_weight):
     current = effect_sizes
-    targets_full = lax.all_gather(targets, "snp", axis=0, tiled=True)
+    length = lax.axis_size("snp")
+    pairs = [(i, (i + 1) % length) for i in range(length)]
+    back = [(b, a) for a, b in pairs]
+    lower, upper = ([], [])
+    for step in range(length - 1):
+        if step % 2 == 0:
+            lower.append(lax.ppermute(lower[-1] if lower else targets, "snp", pairs))
+        else:
+            upper.append(lax.ppermute(upper[-1] if upper else targets, "snp", back))
+    blocks_2 = jnp.stack([*lower[::-1], targets, *upper])
+    shift = lax.axis_index("snp") - len(lower)
+    blocks_2 = blocks_2[(jnp.arange(length) - shift) % length]
+    targets_full = joined_along(blocks_2, 0)
     current_bf = current.astype(jnp.bfloat16)
     fitted = lax.psum(jnp.dot(genotype, current_bf, preferred_element_type=jnp.float32), "snp")
     residual = (targets_full.astype(jnp.float32) - fitted).astype(jnp.bfloat16)

time: 315 us -> 316 us (level)
  blocking collectives: 32.6 us -> 0 us
  waiting for transfers between devices: 157 us -> 176 us
  starting transfers between devices: 0.57 us -> 16.1 us
    all_gather x1 -> x0, blocking collectives: 32.6 us -> none  [body(): targets_full = lax.all_gather(targets, 'snp', axis=0, tiled=True)]
    ppermute x0 -> x7, starting transfers between devices: none -> 15.6 us  [the longest x3 12.6 us: body(): upper.append(lax.ppermute(upper[-1] if upper else targets, 'snp', back))]
    ppermute x0 -> x7, waiting for transfers between devices: none -> 10.2 us  [the longest x4 8.78 us: body(): lower.append(lax.ppermute(lower[-1] if lower else targets, 'snp', pairs))]
    psum x1, waiting for transfers between devices: 25 us -> 33.4 us  [body(): lax.psum(jnp.dot(genotype, current_bf, preferred_element_type=jnp.float32...]
    unnamed x11 -> x18, local copies, waits for them, and re-layouts: 18.4 us -> 17.7 us
  transfers between devices with their start and end apart: 5 -> 12, of which waited for: 5 -> 8; matrix products, arithmetic and copies ran while one was open for 6% -> 8% of each run, Pallas kernels for 0% -> 0%
where the time goes in v1:
time: 316 us
  waiting for transfers between devices  176 us (56%)
  other arithmetic  40.8 us (13%)
  local copies, waits for them, and re-layouts  35.9 us (11%)
  matrix products  33.9 us (11%)
  starting transfers between devices  16.1 us (5%)
  between operations  13.3 us (4%)
    psum x4, waiting for transfers between devices, shrink_local(): node_sq = lax.psum(partial_sq, 'trait')  132 us
    psum x1, waiting for transfers between devices, body(): lax.psum(jnp.dot(genotype, current_bf, preferred_element_type=jnp.float32...  33.4 us
    reduce_sum x3, other arithmetic, shrink_local(): block_sq = jnp.sum(blocks * blocks, axis=2)  28.6 us
    unnamed x18, local copies, waits for them, and re-layouts  17.7 us
    mul x1, local copies, waits for them, and re-layouts, shrink_local(): value = (blocks * block_factor[:, :, None]).reshape(value.shape)  17.4 us
    ppermute x3, starting transfers between devices, body(): upper.append(lax.ppermute(upper[-1] if upper else targets, 'snp', back))  12.6 us
    mul x1, other arithmetic, shrink_local(): value = (blocks * block_factor[:, :, None]).reshape(value.shape)  12 us
    dot_general x1, matrix products, body(): lax.dot_general(genotype, residual, (((0,), (0,)), ((), ())), preferred_e...  11 us
  transfers between devices with their start and end apart: 12, of which 8 were waited for; matrix products, arithmetic and copies ran while one was open for 8% of the time, Pallas kernels for 0%

profile of v1, /device:TPU:0, one launch (start us, length us, event | category | flops | bytes accessed | tf_op | source)
XLA Modules:
  0.0 315.6 jit_solution(14824154680079157013)
XLA Ops:
  6.5 2.9 collective-permute-start
  9.5 3.1 collective-permute-start.4
  12.6 8.1 %fusion = f32[32,4096]{1,0:T(8,128)} fusion(bf16[32,1024]{1,0:T(8,128)(2,1)S(1)} %copy-done, f32[1024,4096]{1,0:T(8,128)} %param.7), kind=kOutput, calls=%fused_computation.10 | convolution fusion | flops 272629760 | bytes 17367040 | tf_op jit(solution)/shard_map/dot_general | solution.py:56
  20.9 6.7 %collective-permute-done.1 = bf16[4,4096]{1,0:T(4,128)(2,1)S(1)} collective-permute-done((bf16[4,4096]{1,0:T(4,128)(2,1)S(1)}, bf16[4,4096]{1,0:T(4,128)(2,1)S(1)}, u32[]{:S(2)}, u32[]{:S(2)}) %collective-permute-start.1) | collective-permute-done | bytes 32800 | tf_op jit(solution)/shard_map/ppermute | solution.py:48
  27.6 4.8 %collective-permute-start.5 = (bf16[4,4096]{1,0:T(4,128)(2,1)S(1)}, bf16[4,4096]{1,0:T(4,128)(2,1)S(1)}, u32[]{:S(2)}, u32[]{:S(2)}) collective-permute-start(bf16[4,4096]{1,0:T(4,128)(2,1)S(1)} %collective-permute-done.4), channel_id=1, source_target_pairs={{4,0},{8,4},{12,8},{16,12},{20,16},{24,20},{28,24},{0,28},{5,1},{9... | collective-permute-start | bytes 98312 | tf_op jit(solution)/shard_map/ppermute | solution.py:50
  32.4 2.1 collective-permute-done.2
  34.5 17.5 %copy.8 = f32[1024,4096]{0,1:T(8,128)} copy(f32[1024,4096]{1,0:T(8,128)} %param.7) | data formatting | bytes 33554432 | tf_op args[2]
  52.0 4.7 %collective-permute-start.6 = (bf16[4,4096]{1,0:T(4,128)(2,1)S(1)}, bf16[4,4096]{1,0:T(4,128)(2,1)S(1)}, u32[]{:S(2)}, u32[]{:S(2)}) collective-permute-start(bf16[4,4096]{1,0:T(4,128)(2,1)S(1)} %collective-permute-done.5), channel_id=1, source_target_pairs={{4,0},{8,4},{12,8},{16,12},{20,16},{24,20},{28,24},{0,28},{5,1},{9... | collective-permute-start | bytes 98312 | tf_op jit(solution)/shard_map/ppermute | solution.py:50
  59.2 33.4 %all-reduce.6.cloned.1.call-done = f32[32,4096]{1,0:T(8,128)} async-done(((f32[32,4096]{1,0:T(8,128)}), f32[32,4096]{1,0:T(8,128)}) %all-reduce.6.cloned.1.call-update) | async-done | bytes 524304 | tf_op jit(solution)/shard_map/psum | solution.py:56
  92.5 11.0 %multiply_reduce_fusion.3 = (f32[1024,32]{0,1:T(8,128)S(1)}, f32[1024,4096]{0,1:T(8,128)}) fusion(f32[1024,4096]{0,1:T(8,128)} %copy.8, bf16[32,1024]{1,0:T(8,128)(2,1)S(1)} %copy-done, f32[32,4096]{1,0:T(8,128)S(1)} %reshape.145, f32[32,4096]{1,0:T(8,128)} %all-reduce.6.cloned.1.call-done), kind=kOutput, calls=%fused_computation.9 | convolution fusion | flops 285442048 | bytes 34799616 | tf_op jit(solution)/shard_map/dot_general | solution.py:58
  103.5 1.8 fusion.24
  105.6 32.4 %all-reduce.8.cloned.1.call-done = f32[1024,128]{1,0:T(8,128)} async-done(((f32[1024,128]{1,0:T(8,128)}), f32[1024,128]{1,0:T(8,128)}) %all-reduce.8.cloned.1.call-update) | async-done | bytes 524304 | tf_op jit(solution)/shard_map/psum | solution.py:33
  139.9 8.5 %multiply_reduce_fusion.2 = f32[1024,32]{0,1:T(8,128)S(1)} fusion(f32[1024,4096]{0,1:T(8,128)} %get-tuple-element.18, f32[1024,32]{0,1:T(8,128)S(1)} %fusion.2), kind=kLoop, calls=%fused_computation.8 | loop fusion | flops 12550144 | bytes 17039360 | tf_op jit(solution)/shard_map/reduce_sum | solution.py:31
  148.4 1.9 fusion.21
  150.5 33.1 %all-reduce.10.cloned.1.call-done = f32[1024,128]{1,0:T(8,128)} async-done(((f32[1024,128]{1,0:T(8,128)}), f32[1024,128]{1,0:T(8,128)}) %all-reduce.10.cloned.1.call-update) | async-done | bytes 524304 | tf_op jit(solution)/shard_map/psum | solution.py:33
  185.4 9.5 %multiply_reduce_fusion.1 = f32[1024,32]{0,1:T(8,128)S(1)} fusion(f32[1024,4096]{0,1:T(8,128)} %get-tuple-element.18, f32[1024,32]{0,1:T(8,128)S(1)} %fusion.3, f32[1024,32]{0,1:T(8,128)S(1)} %fusion.2), kind=kLoop, calls=%fused_computation.7 | loop fusion | flops 16744448 | bytes 17170432 | tf_op jit(solution)/shard_map/reduce_sum | solution.py:31
  194.9 1.9 fusion.18
  197.1 33.1 %all-reduce.12.cloned.1.call-done = f32[1024,128]{1,0:T(8,128)} async-done(((f32[1024,128]{1,0:T(8,128)}), f32[1024,128]{1,0:T(8,128)}) %all-reduce.12.cloned.1.call-update) | async-done | bytes 524304 | tf_op jit(solution)/shard_map/psum | solution.py:33
  232.0 10.6 %multiply_reduce_fusion = f32[1024,32]{0,1:T(8,128)S(1)} fusion(f32[1024,4096]{0,1:T(8,128)} %get-tuple-element.18, f32[1024,32]{0,1:T(8,128)S(1)} %fusion.4, f32[1024,32]{0,1:T(8,128)S(1)} %fusion.3, f32[1024,32]{0,1:T(8,128)S(1)} %fusion.2), kind=kLoop, calls=%fused_computation.6 | loop fusion | flops 20938752 | bytes 17301504 | tf_op jit(solution)/shard_map/reduce_sum | solution.py:31
  242.5 1.9 fusion.15
  244.4 33.3 %all-reduce.14.cloned.1.call-done = f32[1024,128]{1,0:T(8,128)} async-done(((f32[1024,128]{1,0:T(8,128)}), f32[1024,128]{1,0:T(8,128)}) %all-reduce.14.cloned.1.call-update) | async-done | bytes 524304 | tf_op jit(solution)/shard_map/psum | solution.py:33
  277.7 1.8 fusion.5
  279.6 12.0 %bitcast_multiply_fusion = f32[1024,4096]{0,1:T(8,128)} fusion(f32[1024,4096]{0,1:T(8,128)} %get-tuple-element.18, f32[1024,32]{0,1:T(8,128)S(1)} %fusion.5, f32[1024,32]{0,1:T(8,128)S(1)} %fusion.4, f32[1024,32]{0,1:T(8,128)S(1)} %fusion.3, f32[1024,32]{0,1:T(8,128)S(1)} %fusion.2), kind=kLoop, calls=%fused_computation.1 | loop fusion | flops 16777216 | bytes 34078720 | tf_op jit(solution)/shard_map/mul | solution.py:36
  291.6 17.4 %copy.9 = f32[1024,4096]{1,0:T(8,128)} copy(f32[1024,4096]{0,1:T(8,128)} %bitcast_multiply_fusion) | data formatting | bytes 33554432 | tf_op jit(solution)/shard_map/mul | solution.py:36
  (46 shorter events, 8.8 us)
Async XLA Ops:
  6.5 6.0 %copy-start = (bf16[32,1024]{1,0:T(8,128)(2,1)S(1)}, bf16[32,1024]{1,0:T(8,128)(2,1)}, u32[]{:S(2)}) copy-start(bf16[32,1024]{1,0:T(8,128)(2,1)} %param.5) | copy-start | bytes 196612
  6.5 14.3 %copy-start.2 = (s32[4,128,128]{2,1,0:T(8,128)S(1)}, s32[4,128,128]{2,1,0:T(8,128)}, u32[]{:S(2)}) copy-start(s32[4,128,128]{2,1,0:T(8,128)} %param.8) | copy-start | bytes 786436
  6.5 86.0 %all-reduce.6.cloned.1.call-start = ((), (), s32[]{:S(2)}) async-start(), calls=%async_computation | async-start | bytes 1048576 | tf_op jit(solution)/shard_map/psum | solution.py:56
  6.5 14.2 %collective-permute-start = (bf16[4,4096]{1,0:T(4,128)(2,1)}, bf16[4,4096]{1,0:T(4,128)(2,1)S(1)}, u32[]{:S(2)}, u32[]{:S(2)}) collective-permute-start(bf16[4,4096]{1,0:T(4,128)(2,1)} %param.6), channel_id=1, source_target_pairs={{0,4},{4,8},{8,12},{12,16},{16,20},{20,24},{24,28},{28,0},{1,5},{5... | collective-permute-start | bytes 98312 | tf_op jit(solution)/shard_map/ppermute | solution.py:48
  9.5 18.1 %collective-permute-start.4 = (bf16[4,4096]{1,0:T(4,128)(2,1)}, bf16[4,4096]{1,0:T(4,128)(2,1)S(1)}, u32[]{:S(2)}, u32[]{:S(2)}) collective-permute-start(bf16[4,4096]{1,0:T(4,128)(2,1)} %param.6), channel_id=1, source_target_pairs={{4,0},{8,4},{12,8},{16,12},{20,16},{24,20},{28,24},{0,28},{5,1},{9... | collective-permute-start | bytes 98312 | tf_op jit(solution)/shard_map/ppermute | solution.py:50
  20.7 117.3 %all-reduce.8.cloned.1.call-start = ((), (), s32[]{:S(2)}) async-start(), calls=%async_computation.1 | async-start | bytes 1048576 | tf_op jit(solution)/shard_map/psum | solution.py:33
  20.8 6.8 %collective-permute-start.1 = (bf16[4,4096]{1,0:T(4,128)(2,1)S(1)}, bf16[4,4096]{1,0:T(4,128)(2,1)S(1)}, u32[]{:S(2)}, u32[]{:S(2)}) collective-permute-start(bf16[4,4096]{1,0:T(4,128)(2,1)S(1)} %collective-permute-done), channel_id=1, source_target_pairs={{0,4},{4,8},{8,12},{12,16},{16,20},{20,24},{24,28},{28,0},{1,5},{5... | collective-permute-start | bytes 98312 | tf_op jit(solution)/shard_map/ppermute | solution.py:48
  27.6 6.9 %collective-permute-start.2 = (bf16[4,4096]{1,0:T(4,128)(2,1)S(1)}, bf16[4,4096]{1,0:T(4,128)(2,1)S(1)}, u32[]{:S(2)}, u32[]{:S(2)}) collective-permute-start(bf16[4,4096]{1,0:T(4,128)(2,1)S(1)} %collective-permute-done.1), channel_id=1, source_target_pairs={{0,4},{4,8},{8,12},{12,16},{16,20},{20,24},{24,28},{28,0},{1,5},{5... | collective-permute-start | bytes 98312 | tf_op jit(solution)/shard_map/ppermute | solution.py:48
  27.6 24.4 %collective-permute-start.5 = (bf16[4,4096]{1,0:T(4,128)(2,1)S(1)}, bf16[4,4096]{1,0:T(4,128)(2,1)S(1)}, u32[]{:S(2)}, u32[]{:S(2)}) collective-permute-start(bf16[4,4096]{1,0:T(4,128)(2,1)S(1)} %collective-permute-done.4), channel_id=1, source_target_pairs={{4,0},{8,4},{12,8},{16,12},{20,16},{24,20},{28,24},{0,28},{5,1},{9... | collective-permute-start | bytes 98312 | tf_op jit(solution)/shard_map/ppermute | solution.py:50
  34.5 22.2 %collective-permute-start.3 = (bf16[4,4096]{1,0:T(4,128)(2,1)S(1)}, bf16[4,4096]{1,0:T(4,128)(2,1)S(1)}, u32[]{:S(2)}, u32[]{:S(2)}) collective-permute-start(bf16[4,4096]{1,0:T(4,128)(2,1)S(1)} %collective-permute-done.2), channel_id=1, source_target_pairs={{0,4},{4,8},{8,12},{12,16},{16,20},{20,24},{24,28},{28,0},{1,5},{5... | collective-permute-start | bytes 98312 | tf_op jit(solution)/shard_map/ppermute | solution.py:48
  34.5 22.3 %copy-start.3 = (bf16[4,4096]{1,0:T(4,128)(2,1)S(1)}, bf16[4,4096]{1,0:T(4,128)(2,1)}, u32[]{:S(2)}) copy-start(bf16[4,4096]{1,0:T(4,128)(2,1)} %param.6) | copy-start | bytes 98308
  52.0 6.3 %collective-permute-start.6 = (bf16[4,4096]{1,0:T(4,128)(2,1)S(1)}, bf16[4,4096]{1,0:T(4,128)(2,1)S(1)}, u32[]{:S(2)}, u32[]{:S(2)}) collective-permute-start(bf16[4,4096]{1,0:T(4,128)(2,1)S(1)} %collective-permute-done.5), channel_id=1, source_target_pairs={{4,0},{8,4},{12,8},{16,12},{20,16},{24,20},{28,24},{0,28},{5,1},{9... | collective-permute-start | bytes 98312 | tf_op jit(solution)/shard_map/ppermute | solution.py:50
  59.1 46.5 %copy-start.4 = (f32[4,128]{1,0:T(4,128)S(1)}, f32[4,128]{1,0:T(4,128)}, u32[]{:S(2)}) copy-start(f32[4,128]{1,0:T(4,128)} %param.9) | copy-start | bytes 6148
  105.4 78.2 %all-reduce.10.cloned.1.call-start = ((), (), s32[]{:S(2)}) async-start(), calls=%async_computation.2 | async-start | bytes 1048576 | tf_op jit(solution)/shard_map/psum | solution.py:33
  150.3 79.8 %all-reduce.12.cloned.1.call-start = ((), (), s32[]{:S(2)}) async-start(), calls=%async_computation.3 | async-start | bytes 1048576 | tf_op jit(solution)/shard_map/psum | solution.py:33
  196.8 80.9 %all-reduce.14.cloned.1.call-start = ((), (), s32[]{:S(2)}) async-start(), calls=%async_computation.4 | async-start | bytes 1048576 | tf_op jit(solution)/shard_map/psum | solution.py:33
  279.6 29.4 %copy-start.1 = (bf16[32,1024]{1,0:T(8,128)(2,1)S(1)}, bf16[32,1024]{1,0:T(8,128)(2,1)}, u32[]{:S(2)}) copy-start(bf16[32,1024]{1,0:T(8,128)(2,1)} %param.5) | copy-start | bytes 196612
Sparse Core Ops, SparseCore 0:
  20.9 71.6 all-reduce.5
  105.5 32.4 all-reduce.7
  150.4 33.1 all-reduce.9
  196.9 33.1 all-reduce.11
  244.5 33.1 all-reduce.13
